TPU v7x, 32 devices: a whole 2x2x4 slice. The times are simulated.
32 devices in a mesh: tile: 8 (over z, y), src: 4 (over x, core).
Axes of the slice: x: 2, y: 2, z: 4, core: 2. Of those that a mesh axis runs over, the one named last changes fastest.
Arguments:
- excitation: bfloat16 [2, 512, 8192], P(None, 'src', 'tile'), may hold values from -6 to 6
- near_blocks: bfloat16 [16, 3, 2, 512, 512], P('tile'), may hold values from -0.02734375 to 0.02734375
- source_basis: bfloat16 [16, 2, 24, 512], P('tile'), may hold values from -0.1875 to 0.1875
- target_basis: bfloat16 [16, 2, 24, 512], P('tile'), may hold values from -0.625 to 0.625
- coupling: bfloat16 [2, 384, 384], P(None, None, 'tile'), may hold values from -0.109375 to 0.109375
- pair_rank: int32 [16, 16], P(None, 'tile'), may hold values from 2 to 24
- far_link: int32 [16, 16], P(None, 'tile'), may hold values 0 or 1
- focal_kernel: bfloat16 [2, 64, 8192], P(None, None, 'tile'), may hold values from -0.046875 to 0.046875
- focal_target: float32 [64], replicated, may hold values from 0.3 to 0.9
- focal_owner: int32 [64], replicated, may hold values from 0 to 63, each once
Outputs:
- field: float32 [2, 512, 8192], P(None, 'src', 'tile')
- focal_residual: float32 [64], P('tile')
- adjoint: float32 [2, 512, 8192], P(None, 'src', 'tile')
Inputs may be any that keep to these rules, and one draw needn't show every extreme that they name: `focal_owner`: each focal point has its own slot; slot k belongs to index k // 8 of tile.
All inputs are finite; a program needn't handle non-finite values. No bound on the sum of `far_link` on one device may be relied on, other than what follows from the above.
Results may differ from a plain program's by a relative error of at most 0.006.
Values may be sent and summed in bfloat16 or wider, within the bound.
No kernel may reach another device: no remote copies, remote signals or barrier semaphores. Data moves between devices by JAX's collectives and lax.ppermute only.
A program may use at most 64 MiB of HBM per device.

v0:
```python
import jax
import jax.numpy as jnp
from jax import lax
from jax.sharding import PartitionSpec as P

TILE = 512
RANK = 24
DAMPING = 0.8


def extended(x, sides, width):
    for axis, dim in sides:
        size, length = (lax.axis_size(axis), x.shape[dim])
        up = [(i, (i + 1) % size) for i in range(size)]
        down = [(j, i) for i, j in up]
        last = lax.slice_in_dim(x, length - width, length, axis=dim)
        initial = lax.slice_in_dim(x, 0, width, axis=dim)
        before = lax.ppermute(last, axis, up)
        after = lax.ppermute(initial, axis, down)
        x = jnp.concatenate([before, x, after], axis=dim)
    return x


def plain_dot(left, right, contract):
    return lax.dot_general(
        left, right, (((1,), (contract,)), ((), ())), preferred_element_type=jnp.float32
    )


def complex_dot(left_re, left_im, right_re, right_im, contract):
    real_part = plain_dot(left_re, right_re, contract) - plain_dot(left_im, right_im, contract)
    imag_part = plain_dot(left_re, right_im, contract) + plain_dot(left_im, right_re, contract)
    return (real_part, imag_part)


def per_device(
    excitation,
    near_blocks,
    source_basis,
    target_basis,
    coupling,
    pair_rank,
    far_link,
    focal_kernel,
    focal_target,
    focal_owner,
):
    tile_count = near_blocks.shape[0]
    src_rows = excitation.shape[1]
    tiles = pair_rank.shape[0]
    focal_count = focal_target.shape[0]
    first_tile = lax.axis_index("tile") * tile_count
    global_tiles = first_tile + jnp.arange(tile_count)
    source_tiles = jnp.arange(tiles)[:, None]
    distance = (global_tiles[None, :] - source_tiles) % tiles
    far_pairs = (far_link == 1) & (distance != 0) & (distance != 1) & (distance != tiles - 1)
    levels = jnp.arange(RANK)
    rank_limit = pair_rank[:, None, :, None]
    rank_mask = (
        far_pairs[:, None, :, None]
        & (levels[None, :, None, None] < rank_limit)
        & (levels[None, None, None, :] < rank_limit)
    )
    rank_mask = rank_mask.reshape(tiles * RANK, tile_count * RANK)
    masked = coupling * rank_mask.astype(coupling.dtype)
    flipped = lax.all_to_all(masked, "tile", split_axis=1, concat_axis=2, tiled=True)

    def apply_transpose(field):
        field_bf = field.astype(jnp.bfloat16)
        moved_re = [[], [], []]
        moved_im = [[], [], []]
        proj_re = []
        proj_im = []
        for tile_here in range(tile_count):
            own = field_bf[:, :, tile_here * TILE : (tile_here + 1) * TILE]
            for offset in range(3):
                part_re, part_im = complex_dot(
                    own[0],
                    own[1],
                    near_blocks[tile_here, offset, 0],
                    near_blocks[tile_here, offset, 1],
                    1,
                )
                moved_re[offset].append(part_re)
                moved_im[offset].append(part_im)
            part_re, part_im = complex_dot(
                own[0], own[1], target_basis[tile_here, 0], target_basis[tile_here, 1], 1
            )
            proj_re.append(part_re)
            proj_im.append(part_im)
        moved = [
            jnp.stack([jnp.concatenate(moved_re[k], axis=1), jnp.concatenate(moved_im[k], axis=1)])
            for k in range(3)
        ]
        width = tile_count * TILE
        edges = jnp.concatenate([moved[0][:, :, 0:TILE], moved[2][:, :, width - TILE :]], axis=2)
        arrived = extended(edges.astype(jnp.bfloat16), (("tile", 2),), TILE).astype(edges.dtype)
        from_left = jnp.concatenate(
            [arrived[:, :, 0:TILE], moved[2][:, :, 0 : width - TILE]], axis=2
        )
        from_right = jnp.concatenate(
            [moved[0][:, :, TILE:], arrived[:, :, 3 * TILE : 4 * TILE]], axis=2
        )
        near_part = moved[1] + from_left + from_right
        projected = jnp.stack(
            [jnp.concatenate(proj_re, axis=1), jnp.concatenate(proj_im, axis=1)]
        ).astype(jnp.bfloat16)
        shard_piece = lax.all_gather(projected, "tile", axis=2, tiled=True)
        term_re, term_im = complex_dot(shard_piece[0], shard_piece[1], flipped[0], flipped[1], 1)
        summed_back = jnp.stack([term_re, term_im]).astype(jnp.bfloat16)
        far_re = []
        far_im = []
        for tile_here in range(tile_count):
            piece = summed_back[:, :, tile_here * RANK : (tile_here + 1) * RANK]
            part_re, part_im = complex_dot(
                piece[0], piece[1], source_basis[tile_here, 0], source_basis[tile_here, 1], 0
            )
            far_re.append(part_re)
            far_im.append(part_im)
        far_part = jnp.stack([jnp.concatenate(far_re, axis=1), jnp.concatenate(far_im, axis=1)])
        return field + near_part + far_part

    right_side = excitation.astype(jnp.float32)
    field = right_side
    for update in range(2):
        apply_field_bf = field.astype(jnp.bfloat16)
        padded = extended(apply_field_bf, (("tile", 2),), TILE)
        coeff_re = []
        coeff_im = []
        for apply_tile_here in range(tile_count):
            apply_own = apply_field_bf[:, :, apply_tile_here * TILE : (apply_tile_here + 1) * TILE]
            apply_part_re, apply_part_im = complex_dot(
                apply_own[0],
                apply_own[1],
                source_basis[apply_tile_here, 0],
                source_basis[apply_tile_here, 1],
                1,
            )
            coeff_re.append(apply_part_re)
            coeff_im.append(apply_part_im)
        coeff = jnp.stack(
            [jnp.concatenate(coeff_re, axis=1), jnp.concatenate(coeff_im, axis=1)]
        ).astype(jnp.bfloat16)
        fold_shard_piece = lax.all_gather(coeff, "tile", axis=2, tiled=True)
        fold_term_re, fold_term_im = complex_dot(
            fold_shard_piece[0], fold_shard_piece[1], masked[0], masked[1], 0
        )
        coupled = jnp.stack([fold_term_re, fold_term_im]).astype(jnp.bfloat16)
        out_re = []
        out_im = []
        for apply_tile_here in range(tile_count):
            total_re = jnp.zeros((src_rows, TILE), jnp.float32)
            total_im = jnp.zeros((src_rows, TILE), jnp.float32)
            for apply_offset in range(3):
                window = padded[
                    :,
                    :,
                    (apply_tile_here + apply_offset)
                    * TILE : (apply_tile_here + apply_offset + 1)
                    * TILE,
                ]
                apply_part_re, apply_part_im = complex_dot(
                    window[0],
                    window[1],
                    near_blocks[apply_tile_here, apply_offset, 0],
                    near_blocks[apply_tile_here, apply_offset, 1],
                    0,
                )
                total_re = total_re + apply_part_re
                total_im = total_im + apply_part_im
            apply_piece = coupled[:, :, apply_tile_here * RANK : (apply_tile_here + 1) * RANK]
            apply_part_re, apply_part_im = complex_dot(
                apply_piece[0],
                apply_piece[1],
                target_basis[apply_tile_here, 0],
                target_basis[apply_tile_here, 1],
                0,
            )
            out_re.append(total_re + apply_part_re)
            out_im.append(total_im + apply_part_im)
        added = jnp.stack([jnp.concatenate(out_re, axis=1), jnp.concatenate(out_im, axis=1)])
        field = field + DAMPING * (right_side - (field + added))
    field_bf = field.astype(jnp.bfloat16)
    focal_re, focal_im = complex_dot(field_bf[0], field_bf[1], focal_kernel[0], focal_kernel[1], 1)
    slots_here = focal_count // lax.axis_size("tile")
    first_slot = lax.axis_index("tile") * slots_here
    sources = src_rows * lax.axis_size("src")
    permute = (focal_owner[:, None] == jnp.arange(focal_count)[None, :]).astype(jnp.float32)
    summed_focal = lax.psum(jnp.stack([focal_re, focal_im]), "tile")
    intensity = lax.psum(
        jnp.sum(summed_focal[0] * summed_focal[0] + summed_focal[1] * summed_focal[1], axis=0),
        "src",
    )
    residual_part = jnp.tanh(intensity / (2.0 * sources)) - focal_target
    weights_re = (residual_part * summed_focal[0]).astype(jnp.bfloat16)
    weights_im = (-residual_part * summed_focal[1]).astype(jnp.bfloat16)
    residual_slots = jnp.dot(residual_part, permute, precision=lax.Precision.HIGHEST)
    residual_out = lax.dynamic_slice_in_dim(residual_slots, first_slot, slots_here)
    scale_factor = (tiles * TILE / focal_count) ** 0.5
    term_re, term_im = complex_dot(weights_re, weights_im, focal_kernel[0], focal_kernel[1], 0)
    source_term = jnp.stack([term_re, term_im]) * scale_factor
    adjoint = source_term + DAMPING * (source_term - apply_transpose(source_term))
    return (field, residual_out, adjoint)


def solution(mesh):
    return jax.shard_map(
        per_device,
        mesh=mesh,
        in_specs=(
            P(None, "src", "tile"),
            P("tile", None, None, None, None),
            P("tile", None, None, None),
            P("tile", None, None, None),
            P(None, None, "tile"),
            P(None, "tile"),
            P(None, "tile"),
            P(None, None, "tile"),
            P(),
            P(),
        ),
        out_specs=(P(None, "src", "tile"), P("tile"), P(None, "src", "tile")),
        check_vma=False,
    )
```

profile of v0, /device:TPU:0, one launch (start us, length us, event | category | flops | bytes accessed | tf_op | source)
XLA Modules:
  0.0 293.0 jit_solution(17563514672564382302)
XLA Ops:
  7.2 2.0 fusion.459
  9.1 6.0 %collective-permute-start.1 = (bf16[2,128,512]{2,1,0:T(8,128)(2,1)}, bf16[2,128,512]{2,1,0:T(8,128)(2,1)}, u32[]{:S(2)}, u32[]{:S(2)}) collective-permute-start(bf16[2,128,512]{2,1,0:T(8,128)(2,1)} %get-tuple-element.12), channel_id=1, source_target_pairs={{4,0},{8,4},{12,8},{16,12},{20,16},{24,20},{28,24},{0,28},{5,1},{9... | collective-permute-start | bytes 786440 | tf_op jit(solution)/shard_map/ppermute | solution.py:19
  19.8 6.0 %all-to-all-start = ((bf16[8,2,2304]{2,1,0:T(2,128)(2,1)}), bf16[8,2,2304]{2,1,0:T(2,128)(2,1)S(1)}, u32[]{:S(2)}, u32[]{:S(2)}) async-start(bf16[8,2,2304]{2,1,0:T(2,128)(2,1)} %reshape.84), calls=%async_computation | async-start | bytes 147456 | tf_op jit(solution)/shard_map/all_to_all | solution.py:66
  25.8 1.2 fusion.274
  27.0 1.3 fusion.288
  34.8 31.3 %all_gather.9 = bf16[2,128,384]{1,2,0:T(8,128)(2,1)S(1)} all-gather(bf16[2,128,48]{1,2,0:T(8,128)(2,1)S(1)} %pad_maximum_fusion.6), channel_id=1, replica_groups=mesh['tile'=8,'src'=4] {'tile'}, dimensions={2}, use_global_device_ids=true | all-gather | bytes 221184 | tf_op jit(solution)/shard_map/all_gather | solution.py:144
  66.3 1.3 fusion.94
  67.7 1.3 fusion.112
  69.6 1.3 fusion.130
  70.9 1.3 fusion.148
  83.1 1.2 copy.22
  84.3 1.8 fusion.85
  86.1 1.3 fusion.175
  87.4 1.5 fusion.20
  88.9 1.5 fusion.22
  90.5 1.3 fusion.77
  94.2 1.2 fusion.25
  96.9 30.7 %all_gather.10 = bf16[2,128,384]{1,2,0:T(8,128)(2,1)S(1)} all-gather(bf16[2,128,48]{1,2,0:T(8,128)(2,1)S(1)} %pad_maximum_fusion.7), channel_id=1, replica_groups=mesh['tile'=8,'src'=4] {'tile'}, dimensions={2}, use_global_device_ids=true | all-gather | bytes 221184 | tf_op jit(solution)/shard_map/all_gather | solution.py:144
  131.0 4.0 %collective-permute-start.3 = (bf16[2,128,512]{2,1,0:T(8,128)(2,1)S(1)}, bf16[2,128,512]{2,1,0:T(8,128)(2,1)S(1)}, u32[]{:S(2)}, u32[]{:S(2)}) collective-permute-start(bf16[2,128,512]{2,1,0:T(8,128)(2,1)S(1)} %get-tuple-element.10), channel_id=1, source_target_pairs={{4,0},{8,4},{12,8},{16,12},{20,16},{24,20},{28,24},{0,28},{5,1},{9... | collective-permute-start | bytes 786440 | tf_op jit(solution)/shard_map/ppermute | solution.py:19
  139.2 5.9 %collective-permute-done.2 = bf16[2,128,512]{2,1,0:T(8,128)(2,1)S(1)} collective-permute-done((bf16[2,128,512]{2,1,0:T(8,128)(2,1)S(1)}, bf16[2,128,512]{2,1,0:T(8,128)(2,1)S(1)}, u32[]{:S(2)}, u32[]{:S(2)}) %collective-permute-start.2) | collective-permute-done | bytes 262176 | tf_op jit(solution)/shard_map/ppermute | solution.py:18
  147.0 1.3 fusion.456
  150.1 66.4 %all-reduce.2.cloned.1.call-done = f32[2,128,64]{1,2,0:T(8,128)} async-done(((f32[2,128,64]{1,2,0:T(8,128)}), f32[2,128,64]{1,2,0:T(8,128)}) %all-reduce.2.cloned.1.call-update) | async-done | bytes 65552 | tf_op jit(solution)/shard_map/psum | solution.py:189
  217.4 5.8 %psum.15 = f32[64]{0:T(128)S(1)} all-reduce(f32[64]{0:T(128)S(1)} %add_reduce_fusion), channel_id=1, replica_groups=mesh['tile'=8,'src'=4] {'src'}, use_global_device_ids=true, to_apply=%region_2.3 | all-reduce | flops 64 | bytes 512 | tf_op jit(solution)/shard_map/psum | solution.py:190
  223.2 1.2 fusion.253
  227.9 1.3 fusion.106
  229.2 1.4 fusion.160
  230.6 1.3 fusion.116
  236.1 30.7 %all_gather.11 = bf16[2,128,384]{1,2,0:T(8,128)(2,1)S(1)} all-gather(bf16[2,128,48]{1,2,0:T(8,128)(2,1)S(1)} %pad_maximum_fusion.8), channel_id=1, replica_groups=mesh['tile'=8,'src'=4] {'tile'}, dimensions={2}, use_global_device_ids=true | all-gather | bytes 221184 | tf_op jit(solution)/shard_map/all_gather | solution.py:108
  272.0 3.3 %collective-permute-start.5 = (bf16[2,128,512]{2,1,0:T(8,128)(2,1)S(1)}, bf16[2,128,512]{2,1,0:T(8,128)(2,1)S(1)}, u32[]{:S(2)}, u32[]{:S(2)}) collective-permute-start(bf16[2,128,512]{2,1,0:T(8,128)(2,1)S(1)} %fusion.67), channel_id=1, source_target_pairs={{4,0},{8,4},{12,8},{16,12},{20,16},{24,20},{28,24},{0,28},{5,1},{9... | collective-permute-start | bytes 786440 | tf_op jit(solution)/shard_map/ppermute | solution.py:19
  277.4 2.2 collective-permute-done.5
  279.7 4.8 %collective-permute-done.4 = bf16[2,128,512]{2,1,0:T(8,128)(2,1)S(1)} collective-permute-done((bf16[2,128,512]{2,1,0:T(8,128)(2,1)S(1)}, bf16[2,128,512]{2,1,0:T(8,128)(2,1)S(1)}, u32[]{:S(2)}, u32[]{:S(2)}) %collective-permute-start.4) | collective-permute-done | bytes 262176 | tf_op jit(solution)/shard_map/ppermute | solution.py:18
  284.6 1.6 fusion.61
  (211 shorter events, 52.8 us)
Async XLA Ops:
  7.2 62.5 %copy-start.1 = (bf16[2,128,1024]{2,1,0:T(8,128)(2,1)S(1)}, bf16[2,128,1024]{2,1,0:T(8,128)(2,1)}, u32[]{:S(2)}) copy-start(bf16[2,128,1024]{2,1,0:T(8,128)(2,1)} %param.10) | copy-start | bytes 1572868
  7.2 62.0 %copy-start.2 = (bf16[2,2,24,512]{3,2,1,0:T(8,128)(2,1)S(1)}, bf16[2,2,24,512]{3,2,1,0:T(8,128)(2,1)}, u32[]{:S(2)}) copy-start(bf16[2,2,24,512]{3,2,1,0:T(8,128)(2,1)} %param.13) | copy-start | bytes 294916
  9.1 75.1 %collective-permute-start.1 = (bf16[2,128,512]{2,1,0:T(8,128)(2,1)}, bf16[2,128,512]{2,1,0:T(8,128)(2,1)}, u32[]{:S(2)}, u32[]{:S(2)}) collective-permute-start(bf16[2,128,512]{2,1,0:T(8,128)(2,1)} %get-tuple-element.12), channel_id=1, source_target_pairs={{4,0},{8,4},{12,8},{16,12},{20,16},{24,20},{28,24},{0,28},{5,1},{9... | collective-permute-start | bytes 786440 | tf_op jit(solution)/shard_map/ppermute | solution.py:19
  15.2 70.9 %collective-permute-start = (bf16[2,128,512]{2,1,0:T(8,128)(2,1)}, bf16[2,128,512]{2,1,0:T(8,128)(2,1)}, u32[]{:S(2)}, u32[]{:S(2)}) collective-permute-start(bf16[2,128,512]{2,1,0:T(8,128)(2,1)} %get-tuple-element.11), channel_id=1, source_target_pairs={{0,4},{4,8},{8,12},{12,16},{16,20},{20,24},{24,28},{28,0},{1,5},{5... | collective-permute-start | bytes 786440 | tf_op jit(solution)/shard_map/ppermute | solution.py:18
  19.8 62.4 %all-to-all-start = ((bf16[8,2,2304]{2,1,0:T(2,128)(2,1)}), bf16[8,2,2304]{2,1,0:T(2,128)(2,1)S(1)}, u32[]{:S(2)}, u32[]{:S(2)}) async-start(bf16[8,2,2304]{2,1,0:T(2,128)(2,1)} %reshape.84), calls=%async_computation | async-start | bytes 147456 | tf_op jit(solution)/shard_map/all_to_all | solution.py:66
  25.8 190.7 %all-reduce.2.cloned.1.call-start = ((), (), s32[]{:S(2)}) async-start(), calls=%async_computation.1 | async-start | bytes 131072 | tf_op jit(solution)/shard_map/psum | solution.py:189
  25.8 46.6 %copy-start = (bf16[2,3,2,512,512]{4,3,2,1,0:T(8,128)(2,1)S(1)}, bf16[2,3,2,512,512]{4,3,2,1,0:T(8,128)(2,1)}, u32[]{:S(2)}) copy-start(bf16[2,3,2,512,512]{4,3,2,1,0:T(8,128)(2,1)} %param.11) | copy-start | bytes 18874372
  77.7 14.1 %slice-start = ((s8[6291456]{0:T(1024)(128)(4,1)}), s8[2097152]{0:T(1024)(128)(4,1)S(1)}, s32[]{:S(2)}) async-start(s8[6291456]{0:T(1024)(128)(4,1)} %bitcast.613), calls=%async_computation.2 | async-start | bytes 4194304
  83.1 9.9 %copy-start.6 = (f32[128,512]{1,0:T(8,128)S(1)}, f32[128,512]{1,0:T(8,128)}, u32[]{:S(2)}) copy-start(f32[128,512]{1,0:T(8,128)} %convolution_subtract_fusion.23) | copy-start | bytes 786436
  83.1 9.9 %copy-start.7 = (f32[128,512]{1,0:T(8,128)S(1)}, f32[128,512]{1,0:T(8,128)}, u32[]{:S(2)}) copy-start(f32[128,512]{1,0:T(8,128)} %fusion.3) | copy-start | bytes 786436
  83.1 11.1 %copy-start.4 = (f32[128,512]{1,0:T(8,128)S(1)}, f32[128,512]{1,0:T(8,128)}, u32[]{:S(2)}) copy-start(f32[128,512]{1,0:T(8,128)} %convolution_subtract_fusion.16) | copy-start | bytes 786436
  83.1 11.1 %copy-start.5 = (f32[128,512]{1,0:T(8,128)S(1)}, f32[128,512]{1,0:T(8,128)}, u32[]{:S(2)}) copy-start(f32[128,512]{1,0:T(8,128)} %convolution_subtract_fusion.17) | copy-start | bytes 786436
  83.1 8.8 %slice-start.1 = ((s8[6291456]{0:T(1024)(128)(4,1)}), s8[4194304]{0:T(1024)(128)(4,1)S(1)}, s32[]{:S(2)}) async-start(s8[6291456]{0:T(1024)(128)(4,1)} %bitcast.613), calls=%async_computation.3 | async-start | bytes 8388608
  87.4 8.2 %copy-start.8 = (bf16[2,2,24,512]{3,2,1,0:T(8,128)(2,1)S(1)}, bf16[2,2,24,512]{3,2,1,0:T(8,128)(2,1)}, u32[]{:S(2)}) copy-start(bf16[2,2,24,512]{3,2,1,0:T(8,128)(2,1)} %param.12) | copy-start | bytes 294916
  131.0 7.9 %collective-permute-start.3 = (bf16[2,128,512]{2,1,0:T(8,128)(2,1)S(1)}, bf16[2,128,512]{2,1,0:T(8,128)(2,1)S(1)}, u32[]{:S(2)}, u32[]{:S(2)}) collective-permute-start(bf16[2,128,512]{2,1,0:T(8,128)(2,1)S(1)} %get-tuple-element.10), channel_id=1, source_target_pairs={{4,0},{8,4},{12,8},{16,12},{20,16},{24,20},{28,24},{0,28},{5,1},{9... | collective-permute-start | bytes 786440 | tf_op jit(solution)/shard_map/ppermute | solution.py:19
  136.0 9.1 %collective-permute-start.2 = (bf16[2,128,512]{2,1,0:T(8,128)(2,1)S(1)}, bf16[2,128,512]{2,1,0:T(8,128)(2,1)S(1)}, u32[]{:S(2)}, u32[]{:S(2)}) collective-permute-start(bf16[2,128,512]{2,1,0:T(8,128)(2,1)S(1)} %get-tuple-element.9), channel_id=1, source_target_pairs={{0,4},{4,8},{8,12},{12,16},{16,20},{20,24},{24,28},{28,0},{1,5},{5... | collective-permute-start | bytes 786440 | tf_op jit(solution)/shard_map/ppermute | solution.py:18
  145.9 2.4 copy-start.3
  146.2 77.1 %copy-start.10 = (f32[64]{0:T(128)S(1)}, f32[64]{0:T(128)}, u32[]{:S(2)}) copy-start(f32[64]{0:T(128)} %param.18) | copy-start | bytes 772
  147.0 85.0 %slice-start.2 = ((s8[6291456]{0:T(1024)(128)(4,1)}), s8[2097152]{0:T(1024)(128)(4,1)S(1)}, s32[]{:S(2)}) async-start(s8[6291456]{0:T(1024)(128)(4,1)} %bitcast.615), calls=%async_computation.4 | async-start | bytes 4194304
  223.2 8.7 %slice-start.3 = ((s8[6291456]{0:T(1024)(128)(4,1)}), s8[4194304]{0:T(1024)(128)(4,1)S(1)}, s32[]{:S(2)}) async-start(s8[6291456]{0:T(1024)(128)(4,1)} %bitcast.615), calls=%async_computation.5 | async-start | bytes 8388608
  229.2 38.0 %copy-start.9 = (bf16[2,2,24,512]{3,2,1,0:T(8,128)(2,1)S(1)}, bf16[2,2,24,512]{3,2,1,0:T(8,128)(2,1)}, u32[]{:S(2)}) copy-start(bf16[2,2,24,512]{3,2,1,0:T(8,128)(2,1)} %param.12) | copy-start | bytes 294916
  271.5 5.0 %copy-start.11 = (s32[64]{0:T(128)S(1)}, s32[64]{0:T(128)}, u32[]{:S(2)}) copy-start(s32[64]{0:T(128)} %param.19) | copy-start | bytes 772
  272.0 7.7 %collective-permute-start.5 = (bf16[2,128,512]{2,1,0:T(8,128)(2,1)S(1)}, bf16[2,128,512]{2,1,0:T(8,128)(2,1)S(1)}, u32[]{:S(2)}, u32[]{:S(2)}) collective-permute-start(bf16[2,128,512]{2,1,0:T(8,128)(2,1)S(1)} %fusion.67), channel_id=1, source_target_pairs={{4,0},{8,4},{12,8},{16,12},{20,16},{24,20},{28,24},{0,28},{5,1},{9... | collective-permute-start | bytes 786440 | tf_op jit(solution)/shard_map/ppermute | solution.py:19
  275.4 9.1 %collective-permute-start.4 = (bf16[2,128,512]{2,1,0:T(8,128)(2,1)S(1)}, bf16[2,128,512]{2,1,0:T(8,128)(2,1)S(1)}, u32[]{:S(2)}, u32[]{:S(2)}) collective-permute-start(bf16[2,128,512]{2,1,0:T(8,128)(2,1)S(1)} %fusion.69), channel_id=1, source_target_pairs={{0,4},{4,8},{8,12},{12,16},{16,20},{20,24},{24,28},{28,0},{1,5},{5... | collective-permute-start | bytes 786440 | tf_op jit(solution)/shard_map/ppermute | solution.py:18
Sparse Core Ops, SparseCore 0:
  150.0 66.4 all-reduce.1
where the time goes:
time: 294 us; the launch traced here: 293 us
  blocking collectives  98.5 us (34%)
  waiting for transfers between devices  80.4 us (27%)
  matrix products  64.3 us (22%)
  starting transfers between devices  19.5 us (7%)
  between operations  15.3 us (5%)
  other arithmetic  8.67 us (3%)
  local copies, waits for them, and re-layouts  6.31 us (2%)
    psum x1, waiting for transfers between devices, per_device(): summed_focal = lax.psum(jnp.stack([focal_re, focal_im]), 'tile')  66.4 us
    dot_general x140, matrix products, plain_dot(): lax.dot_general(left, right, (((1,), (contract,)), ((), ())), preferred_e...  64.1 us
    all_gather x2, blocking collectives, per_device(): fold_shard_piece = lax.all_gather(coeff, 'tile', axis=2, tiled=True)  62 us
    all_gather x1, blocking collectives, apply_transpose(): shard_piece = lax.all_gather(projected, 'tile', axis=2, tiled=True)  30.7 us
    ppermute x3, starting transfers between devices, extended(): after = lax.ppermute(initial, axis, down)  13.3 us
    ppermute x3, waiting for transfers between devices, extended(): before = lax.ppermute(last, axis, up)  10.7 us
    all_to_all x1, starting transfers between devices, per_device(): lax.all_to_all(masked, 'tile', split_axis=1, concat_axis=2, tiled=True)  6 us
  transfers between devices with their start and end apart: 8, of which 5 were waited for; matrix products, arithmetic and copies ran while one was open for 13% of the time, Pallas kernels for 0%

commit v1 on v0

--- a/solution.py
+++ b/solution.py
@@ -186,7 +186,7 @@
     first_slot = lax.axis_index("tile") * slots_here
     sources = src_rows * lax.axis_size("src")
     permute = (focal_owner[:, None] == jnp.arange(focal_count)[None, :]).astype(jnp.float32)
-    summed_focal = lax.psum(jnp.stack([focal_re, focal_im]), "tile")
+    summed_focal = jnp.sum(lax.all_gather(jnp.stack([focal_re, focal_im]), "tile"), axis=0)
     intensity = lax.psum(
         jnp.sum(summed_focal[0] * summed_focal[0] + summed_focal[1] * summed_focal[1], axis=0),
         "src",

time: 294 us -> 238 us (0.81)
  waiting for transfers between devices: 80.4 us -> 13.3 us
  blocking collectives: 98.5 us -> 130 us
  between operations: 15.3 us -> 1.93 us
  matrix products: 64.3 us -> 61.1 us
    psum x1 -> x0, waiting for transfers between devices: 66.4 us -> none  [per_device(): summed_focal = lax.psum(jnp.stack([focal_re, focal_im]), 'tile')]
    all_gather x0 -> x1, blocking collectives: none -> 31.4 us  [per_device(): lax.all_gather(jnp.stack([focal_re, focal_im]), 'tile')]
    dot_general x140, matrix products: 64.1 us -> 60.9 us  [plain_dot(): lax.dot_general(left, right, (((1,), (contract,)), ((), ())), preferred_e...]
  transfers between devices with their start and end apart: 8 -> 7, of which waited for: 5 -> 4; matrix products, arithmetic and copies ran while one was open for 13% -> 16% of each run, Pallas kernels for 0% -> 0%
where the time goes in v1:
time: 238 us; the launch traced here: 237 us
  blocking collectives  130 us (55%)
  matrix products  61.1 us (26%)
  starting transfers between devices  18.3 us (8%)
  waiting for transfers between devices  13.3 us (6%)
  other arithmetic  7.3 us (3%)
  local copies, waits for them, and re-layouts  5.4 us (2%)
    all_gather x2, blocking collectives, per_device(): fold_shard_piece = lax.all_gather(coeff, 'tile', axis=2, tiled=True)  62 us
    dot_general x140, matrix products, plain_dot(): lax.dot_general(left, right, (((1,), (contract,)), ((), ())), preferred_e...  60.9 us
    all_gather x1, blocking collectives, per_device(): lax.all_gather(jnp.stack([focal_re, focal_im]), 'tile')  31.4 us
    all_gather x1, blocking collectives, apply_transpose(): shard_piece = lax.all_gather(projected, 'tile', axis=2, tiled=True)  30.6 us
    ppermute x3, starting transfers between devices, extended(): after = lax.ppermute(initial, axis, down)  11 us
    ppermute x3, waiting for transfers between devices, extended(): before = lax.ppermute(last, axis, up)  9.73 us
    all_to_all x1, starting transfers between devices, per_device(): lax.all_to_all(masked, 'tile', split_axis=1, concat_axis=2, tiled=True)  6 us
    psum x1, blocking collectives, per_device(): lax.psum(jnp.sum(summed_focal[0] * summed_focal[0] + summed_focal[1] * su...  5.85 us
  transfers between devices with their start and end apart: 7, of which 4 were waited for; matrix products, arithmetic and copies ran while one was open for 16% of the time, Pallas kernels for 0%

profile of v1, /device:TPU:0, one launch (start us, length us, event | category | flops | bytes accessed | tf_op | source)
XLA Modules:
  0.0 237.2 jit_solution(13388173700304325301)
XLA Ops:
  0.7 1.9 fusion.459
  2.6 6.0 %collective-permute-start.1 = (bf16[2,128,512]{2,1,0:T(8,128)(2,1)}, bf16[2,128,512]{2,1,0:T(8,128)(2,1)}, u32[]{:S(2)}, u32[]{:S(2)}) collective-permute-start(bf16[2,128,512]{2,1,0:T(8,128)(2,1)} %get-tuple-element.12), channel_id=1, source_target_pairs={{4,0},{8,4},{12,8},{16,12},{20,16},{24,20},{28,24},{0,28},{5,1},{9... | collective-permute-start | bytes 786440 | tf_op jit(solution)/shard_map/ppermute | solution.py:19
  13.2 6.0 %all-to-all-start = ((bf16[8,2,2304]{2,1,0:T(2,128)(2,1)}), bf16[8,2,2304]{2,1,0:T(2,128)(2,1)}, u32[]{:S(2)}, u32[]{:S(2)}) async-start(bf16[8,2,2304]{2,1,0:T(2,128)(2,1)} %reshape.85), calls=%async_computation | async-start | bytes 147456 | tf_op jit(solution)/shard_map/all_to_all | solution.py:66
  19.2 1.2 fusion.274
  20.4 1.3 fusion.288
  28.2 31.3 %all_gather.15 = bf16[2,128,384]{1,2,0:T(8,128)(2,1)S(1)} all-gather(bf16[2,128,48]{1,2,0:T(8,128)(2,1)S(1)} %pad_maximum_fusion.6), channel_id=1, replica_groups=mesh['tile'=8,'src'=4] {'tile'}, dimensions={2}, use_global_device_ids=true | all-gather | bytes 221184 | tf_op jit(solution)/shard_map/all_gather | solution.py:144
  59.8 1.3 fusion.94
  61.1 1.3 fusion.112
  63.1 1.3 fusion.130
  64.3 1.3 fusion.148
  77.1 1.5 fusion.85
  78.6 1.6 fusion.175
  80.2 1.5 fusion.20
  81.7 1.5 fusion.22
  83.2 1.3 fusion.77
  84.6 1.3 fusion.167
  87.2 1.2 fusion.25
  89.9 30.7 %all_gather.16 = bf16[2,128,384]{1,2,0:T(8,128)(2,1)S(1)} all-gather(bf16[2,128,48]{1,2,0:T(8,128)(2,1)S(1)} %pad_maximum_fusion.7), channel_id=1, replica_groups=mesh['tile'=8,'src'=4] {'tile'}, dimensions={2}, use_global_device_ids=true | all-gather | bytes 221184 | tf_op jit(solution)/shard_map/all_gather | solution.py:144
  124.0 4.0 %collective-permute-start.3 = (bf16[2,128,512]{2,1,0:T(8,128)(2,1)S(1)}, bf16[2,128,512]{2,1,0:T(8,128)(2,1)S(1)}, u32[]{:S(2)}, u32[]{:S(2)}) collective-permute-start(bf16[2,128,512]{2,1,0:T(8,128)(2,1)S(1)} %get-tuple-element.10), channel_id=1, source_target_pairs={{4,0},{8,4},{12,8},{16,12},{20,16},{24,20},{28,24},{0,28},{5,1},{9... | collective-permute-start | bytes 786440 | tf_op jit(solution)/shard_map/ppermute | solution.py:19
  130.9 1.4 collective-permute-done.3
  132.5 6.0 %collective-permute-done.2 = bf16[2,128,512]{2,1,0:T(8,128)(2,1)S(1)} collective-permute-done((bf16[2,128,512]{2,1,0:T(8,128)(2,1)S(1)}, bf16[2,128,512]{2,1,0:T(8,128)(2,1)S(1)}, u32[]{:S(2)}, u32[]{:S(2)}) %collective-permute-start.2) | collective-permute-done | bytes 262176 | tf_op jit(solution)/shard_map/ppermute | solution.py:18
  140.4 1.3 fusion.456
  142.6 31.4 %all-gather = f32[16,128,64]{1,2,0:T(8,128)S(1)} all-gather(f32[2,128,64]{1,2,0:T(8,128)S(1)} %pad_maximum_fusion.5), channel_id=2, replica_groups=mesh['tile'=8,'src'=4] {'tile'}, dimensions={0}, use_global_device_ids=true | all-gather | bytes 589824 | tf_op jit(solution)/shard_map/all_gather | solution.py:189
  174.2 5.8 %psum.7 = f32[64]{0:T(128)S(1)} all-reduce(f32[64]{0:T(128)S(1)} %add_reduce_fusion), channel_id=1, replica_groups=mesh['tile'=8,'src'=4] {'src'}, use_global_device_ids=true, to_apply=%region_2.3 | all-reduce | flops 64 | bytes 512 | tf_op jit(solution)/shard_map/psum | solution.py:190
  181.4 1.3 fusion.106
  182.8 1.3 fusion.160
  184.1 1.3 fusion.116
  189.6 30.6 %all_gather.19 = bf16[2,128,384]{1,2,0:T(8,128)(2,1)S(1)} all-gather(bf16[2,128,48]{1,2,0:T(8,128)(2,1)S(1)} %pad_maximum_fusion.8), channel_id=1, replica_groups=mesh['tile'=8,'src'=4] {'tile'}, dimensions={2}, use_global_device_ids=true | all-gather | bytes 221184 | tf_op jit(solution)/shard_map/all_gather | solution.py:108
  226.4 1.2 collective-permute-start.4
  229.7 2.2 collective-permute-done.5
  231.8 3.7 %collective-permute-done.4 = bf16[2,128,512]{2,1,0:T(8,128)(2,1)S(1)} collective-permute-done((bf16[2,128,512]{2,1,0:T(8,128)(2,1)S(1)}, bf16[2,128,512]{2,1,0:T(8,128)(2,1)S(1)}, u32[]{:S(2)}, u32[]{:S(2)}) %collective-permute-start.4) | collective-permute-done | bytes 262176 | tf_op jit(solution)/shard_map/ppermute | solution.py:18
  235.7 1.6 fusion.61
  (208 shorter events, 48.3 us)
Async XLA Ops:
  0.6 62.4 %copy-start.1 = (bf16[2,128,1024]{2,1,0:T(8,128)(2,1)S(1)}, bf16[2,128,1024]{2,1,0:T(8,128)(2,1)}, u32[]{:S(2)}) copy-start(bf16[2,128,1024]{2,1,0:T(8,128)(2,1)} %param.10) | copy-start | bytes 1572868
  0.6 62.0 %copy-start.2 = (bf16[2,2,24,512]{3,2,1,0:T(8,128)(2,1)S(1)}, bf16[2,2,24,512]{3,2,1,0:T(8,128)(2,1)}, u32[]{:S(2)}) copy-start(bf16[2,2,24,512]{3,2,1,0:T(8,128)(2,1)} %param.13) | copy-start | bytes 294916
  2.6 74.5 %collective-permute-start.1 = (bf16[2,128,512]{2,1,0:T(8,128)(2,1)}, bf16[2,128,512]{2,1,0:T(8,128)(2,1)}, u32[]{:S(2)}, u32[]{:S(2)}) collective-permute-start(bf16[2,128,512]{2,1,0:T(8,128)(2,1)} %get-tuple-element.12), channel_id=1, source_target_pairs={{4,0},{8,4},{12,8},{16,12},{20,16},{24,20},{28,24},{0,28},{5,1},{9... | collective-permute-start | bytes 786440 | tf_op jit(solution)/shard_map/ppermute | solution.py:19
  8.6 70.0 %collective-permute-start = (bf16[2,128,512]{2,1,0:T(8,128)(2,1)}, bf16[2,128,512]{2,1,0:T(8,128)(2,1)}, u32[]{:S(2)}, u32[]{:S(2)}) collective-permute-start(bf16[2,128,512]{2,1,0:T(8,128)(2,1)} %get-tuple-element.11), channel_id=1, source_target_pairs={{0,4},{4,8},{8,12},{12,16},{16,20},{20,24},{24,28},{28,0},{1,5},{5... | collective-permute-start | bytes 786440 | tf_op jit(solution)/shard_map/ppermute | solution.py:18
  13.2 62.4 %all-to-all-start = ((bf16[8,2,2304]{2,1,0:T(2,128)(2,1)}), bf16[8,2,2304]{2,1,0:T(2,128)(2,1)}, u32[]{:S(2)}, u32[]{:S(2)}) async-start(bf16[8,2,2304]{2,1,0:T(2,128)(2,1)} %reshape.85), calls=%async_computation | async-start | bytes 147456 | tf_op jit(solution)/shard_map/all_to_all | solution.py:66
  19.2 46.6 %copy-start = (bf16[2,3,2,512,512]{4,3,2,1,0:T(8,128)(2,1)S(1)}, bf16[2,3,2,512,512]{4,3,2,1,0:T(8,128)(2,1)}, u32[]{:S(2)}) copy-start(bf16[2,3,2,512,512]{4,3,2,1,0:T(8,128)(2,1)} %param.11) | copy-start | bytes 18874372
  71.6 14.4 %slice-start = ((s8[6291456]{0:T(1024)(128)(4,1)}), s8[2097152]{0:T(1024)(128)(4,1)S(1)}, s32[]{:S(2)}) async-start(s8[6291456]{0:T(1024)(128)(4,1)} %bitcast.614), calls=%async_computation.1 | async-start | bytes 4194304
  77.0 8.9 %slice-start.1 = ((s8[6291456]{0:T(1024)(128)(4,1)}), s8[4194304]{0:T(1024)(128)(4,1)S(1)}, s32[]{:S(2)}) async-start(s8[6291456]{0:T(1024)(128)(4,1)} %bitcast.614), calls=%async_computation.2 | async-start | bytes 8388608
  77.1 8.9 %copy-start.6 = (f32[128,512]{1,0:T(8,128)S(1)}, f32[128,512]{1,0:T(8,128)}, u32[]{:S(2)}) copy-start(f32[128,512]{1,0:T(8,128)} %convolution_subtract_fusion.23) | copy-start | bytes 786436
  77.1 8.9 %copy-start.7 = (f32[128,512]{1,0:T(8,128)S(1)}, f32[128,512]{1,0:T(8,128)}, u32[]{:S(2)}) copy-start(f32[128,512]{1,0:T(8,128)} %fusion.3) | copy-start | bytes 786436
  77.1 10.1 %copy-start.4 = (f32[128,512]{1,0:T(8,128)S(1)}, f32[128,512]{1,0:T(8,128)}, u32[]{:S(2)}) copy-start(f32[128,512]{1,0:T(8,128)} %convolution_subtract_fusion.16) | copy-start | bytes 786436
  77.1 10.1 %copy-start.5 = (f32[128,512]{1,0:T(8,128)S(1)}, f32[128,512]{1,0:T(8,128)}, u32[]{:S(2)}) copy-start(f32[128,512]{1,0:T(8,128)} %convolution_subtract_fusion.17) | copy-start | bytes 786436
  80.2 8.4 %copy-start.8 = (bf16[2,2,24,512]{3,2,1,0:T(8,128)(2,1)S(1)}, bf16[2,2,24,512]{3,2,1,0:T(8,128)(2,1)}, u32[]{:S(2)}) copy-start(bf16[2,2,24,512]{3,2,1,0:T(8,128)(2,1)} %param.12) | copy-start | bytes 294916
  124.0 8.3 %collective-permute-start.3 = (bf16[2,128,512]{2,1,0:T(8,128)(2,1)S(1)}, bf16[2,128,512]{2,1,0:T(8,128)(2,1)S(1)}, u32[]{:S(2)}, u32[]{:S(2)}) collective-permute-start(bf16[2,128,512]{2,1,0:T(8,128)(2,1)S(1)} %get-tuple-element.10), channel_id=1, source_target_pairs={{4,0},{8,4},{12,8},{16,12},{20,16},{24,20},{28,24},{0,28},{5,1},{9... | collective-permute-start | bytes 786440 | tf_op jit(solution)/shard_map/ppermute | solution.py:19
  129.0 9.6 %collective-permute-start.2 = (bf16[2,128,512]{2,1,0:T(8,128)(2,1)S(1)}, bf16[2,128,512]{2,1,0:T(8,128)(2,1)S(1)}, u32[]{:S(2)}, u32[]{:S(2)}) collective-permute-start(bf16[2,128,512]{2,1,0:T(8,128)(2,1)S(1)} %get-tuple-element.9), channel_id=1, source_target_pairs={{0,4},{4,8},{8,12},{12,16},{16,20},{20,24},{24,28},{28,0},{1,5},{5... | collective-permute-start | bytes 786440 | tf_op jit(solution)/shard_map/ppermute | solution.py:18
  139.3 2.4 %copy-start.3 = (bf16[2,64,1024]{2,1,0:T(8,128)(2,1)S(1)}, bf16[2,64,1024]{2,1,0:T(8,128)(2,1)}, u32[]{:S(2)}) copy-start(bf16[2,64,1024]{2,1,0:T(8,128)(2,1)} %param.17) | copy-start | bytes 786436
  139.8 40.2 %copy-start.9 = (f32[64]{0:T(128)S(1)}, f32[64]{0:T(128)}, u32[]{:S(2)}) copy-start(f32[64]{0:T(128)} %param.18) | copy-start | bytes 772
  140.4 45.1 %slice-start.2 = ((s8[6291456]{0:T(1024)(128)(4,1)}), s8[2097152]{0:T(1024)(128)(4,1)S(1)}, s32[]{:S(2)}) async-start(s8[6291456]{0:T(1024)(128)(4,1)} %bitcast.616), calls=%async_computation.3 | async-start | bytes 4194304
  180.0 5.5 %slice-start.3 = ((s8[6291456]{0:T(1024)(128)(4,1)}), s8[4194304]{0:T(1024)(128)(4,1)S(1)}, s32[]{:S(2)}) async-start(s8[6291456]{0:T(1024)(128)(4,1)} %bitcast.616), calls=%async_computation.4 | async-start | bytes 8388608
  225.0 3.8 %copy-start.10 = (s32[64]{0:T(128)S(1)}, s32[64]{0:T(128)}, u32[]{:S(2)}) copy-start(s32[64]{0:T(128)} %param.19) | copy-start | bytes 772
  225.4 6.4 %collective-permute-start.5 = (bf16[2,128,512]{2,1,0:T(8,128)(2,1)S(1)}, bf16[2,128,512]{2,1,0:T(8,128)(2,1)S(1)}, u32[]{:S(2)}, u32[]{:S(2)}) collective-permute-start(bf16[2,128,512]{2,1,0:T(8,128)(2,1)S(1)} %fusion.67), channel_id=1, source_target_pairs={{4,0},{8,4},{12,8},{16,12},{20,16},{24,20},{28,24},{0,28},{5,1},{9... | collective-permute-start | bytes 786440 | tf_op jit(solution)/shard_map/ppermute | solution.py:19
  226.4 9.1 %collective-permute-start.4 = (bf16[2,128,512]{2,1,0:T(8,128)(2,1)S(1)}, bf16[2,128,512]{2,1,0:T(8,128)(2,1)S(1)}, u32[]{:S(2)}, u32[]{:S(2)}) collective-permute-start(bf16[2,128,512]{2,1,0:T(8,128)(2,1)S(1)} %fusion.69), channel_id=1, source_target_pairs={{0,4},{4,8},{8,12},{12,16},{16,20},{20,24},{24,28},{28,0},{1,5},{5... | collective-permute-start | bytes 786440 | tf_op jit(solution)/shard_map/ppermute | solution.py:18
